TPU v7x, 512 devices: a whole 4x8x8 slice. The times are simulated.
512 devices in a mesh: row: 8 (over y), col: 64 (over z, x, core).
Axes of the slice: x: 4, y: 8, z: 8, core: 2. Of those that a mesh axis runs over, the one named last changes fastest.
Arguments:
- ppmi: bfloat16 [4096, 128256], P('row', 'col'), may hold values from -12000 to 12000
- basis: bfloat16 [256, 128256], P(None, 'col'), may hold values from -10 to 10
Outputs:
- left_basis: bfloat16 [256, 4096], P(None, 'row')
- right_basis: bfloat16 [256, 128256], P(None, 'col')
All inputs are finite; a program needn't handle non-finite values.
Results may differ from a plain program's by a relative error of at most 0.0045.
Values may be sent and summed in bfloat16 or wider, within the bound.
A program may use at most 128 MiB of HBM per device.

v0:
```python
import jax
import jax.numpy as jnp
from jax import lax
from jax.sharding import Mesh
from jax.sharding import PartitionSpec as P

COL = ("col_0", "col_1", "col_2")


def in_blocks(array, dim, peers):
    before, after = (array.shape[:dim], array.shape[dim + 1 :])
    return jnp.moveaxis(array.reshape(*before, peers, -1, *after), dim, 0)


def sum_at_owner(array, axis, dim):
    peers = lax.axis_size(axis)
    pieces = lax.all_to_all(in_blocks(array, dim, peers), axis, 0, 0, tiled=True)
    return jnp.sum(pieces, axis=0)


def summed_rows(array, axes, dim):
    far, near = axes
    pieces = in_blocks(array, dim, lax.axis_size(far))
    nearer = sum_at_owner(pieces, near, dim + 1)
    arrived = lax.all_to_all(nearer, far, split_axis=0, concat_axis=0, tiled=True)
    return arrived.sum(axis=0)


def rows_for(lines, peers):
    spare = -len(lines) % peers
    return jnp.pad(lines, [(0, spare)] + [(0, 0)] * (lines.ndim - 1))


def copy_for_each(array, axis):
    peers = lax.axis_size(axis)
    return lax.all_to_all(
        jnp.broadcast_to(array[None], (peers, *array.shape)), axis, 0, 0, tiled=True
    )


def joined_along(pieces, dim):
    shape = list(pieces.shape[1:])
    shape[dim] *= pieces.shape[0]
    return jnp.moveaxis(pieces, 0, dim).reshape(shape)


def gathered_by_axis(array, axes, dim):
    far, near = axes
    pieces = copy_for_each(copy_for_each(array, far), near)
    return joined_along(pieces.swapaxes(0, 1).reshape(-1, *array.shape), dim)


def nested_sum(array, axes):
    lines = array.reshape(-1, array.shape[-1])
    own = summed_rows(rows_for(lines, lax.axis_size(axes[0]) * lax.axis_size(axes[1])), axes, 0)
    whole = gathered_by_axis(own, axes, 0)
    return whole[: len(lines)].reshape(array.shape)


def of_everyone(array, axis):
    everything = copy_for_each(array, axis)
    return jnp.sum(everything, axis=0)


def local_gram(block):
    return jnp.dot(block, block.T, precision=lax.Precision.HIGHEST)


def solve_rows(gram, block):
    lower = jnp.linalg.cholesky(gram)
    solved = lax.linalg.triangular_solve(lower, block, left_side=True, lower=True)
    return solved.astype(jnp.bfloat16)


def local(ppmi, basis):
    rows_total = ppmi.shape[0] * lax.axis_size("row")
    cols_total = ppmi.shape[1] * lax.axis_size(COL)
    basis_now = basis
    left = None
    partial_value = lax.dot_general(
        basis_now, ppmi, (((1,), (1,)), ((), ())), preferred_element_type=jnp.float32
    )
    y_total = nested_sum(partial_value, (("col_0", "col_1"), "col_2"))
    gram_left = of_everyone(local_gram(y_total), "row") / rows_total
    left = solve_rows(gram_left, y_total)
    z_part = jnp.dot(left, ppmi, preferred_element_type=jnp.float32)
    z_total = lax.psum(z_part, "row")
    gram_right = nested_sum(local_gram(z_total), (("col_0", "col_1"), "col_2")) / cols_total
    basis_now = solve_rows(gram_right, z_total)
    return (left, basis_now)


def solution(mesh):
    split = Mesh(
        mesh.devices.reshape(mesh.shape["row"], 8, 4, 2), ("row", "col_0", "col_1", "col_2")
    )
    placed = (P("row", COL), P(None, COL))
    return jax.shard_map(
        local,
        mesh=split,
        in_specs=placed,
        out_specs=(P(None, "row"), P(None, COL)),
        check_vma=False,
    )
```

profile of v0, /device:TPU:1, one launch (start us, length us, event | category | flops | bytes accessed | tf_op | source)
XLA Modules:
  0.0 394.9 jit_solution(5545338627759966449)
XLA Ops:
  7.2 1.6 copy-done
  8.7 1.9 fusion.18
  10.8 0.8 copy.40
  11.7 10.4 %all-to-all-start = ((f32[2,32,4,512]{3,2,1,0:T(4,128)}), f32[2,32,4,512]{3,2,1,0:T(4,128)S(1)}, u32[]{:S(2)}, u32[]{:S(2)}) async-start(f32[2,32,4,512]{3,2,1,0:T(4,128)} %bitcast.70), calls=%async_computation | async-start | bytes 1048576 | tf_op jit(solution)/shard_map/all_to_all | solution.py:17
  22.0 1.4 all-to-all-done
  23.6 18.9 %all_to_all.49 = f32[32,4,512]{2,1,0:T(4,128)S(1)} all-to-all(f32[32,4,512]{2,1,0:T(4,128)S(1)} %reduce_sum.45), channel_id=1, replica_groups=mesh['row'=8,'col_0'=8,'col_1'=4,'col_2'=2] {'col_0','col_1'}, dimensions={0} | all-to-all | bytes 524288 | tf_op jit(solution)/shard_map/all_to_all | solution.py:25
  42.6 15.0 %all_to_all.45 = f32[32,4,512]{2,1,0:T(4,128)S(1)} all-to-all(f32[32,4,512]{2,1,0:T(4,128)S(1)} %broadcast_in_dim.10), channel_id=1, replica_groups=mesh['row'=8,'col_0'=8,'col_1'=4,'col_2'=2] {'col_0','col_1'}, dimensions={0} | all-to-all | bytes 524288 | tf_op jit(solution)/shard_map/all_to_all | solution.py:36
  57.7 7.1 %all_to_all.46 = f32[2,32,4,512]{3,2,1,0:T(4,128)S(1)} all-to-all(f32[2,32,4,512]{3,2,1,0:T(4,128)S(1)} %broadcast_in_dim.11), channel_id=1, replica_groups=mesh['row'=8,'col_0'=8,'col_1'=4,'col_2'=2] {'col_2'}, dimensions={0} | all-to-all | bytes 1048576 | tf_op jit(solution)/shard_map/all_to_all | solution.py:36
  64.7 0.9 copy.27
  65.6 1.2 reshape_reshape.11
  66.8 0.6 fusion.19
  67.5 1.5 broadcast_in_dim.12
  68.9 6.8 %all-to-all-start.4 = ((f32[8,256,256]{2,1,0:T(8,128)}), f32[8,256,256]{2,1,0:T(8,128)}, u32[]{:S(2)}, u32[]{:S(2)}) async-start(f32[8,256,256]{2,1,0:T(8,128)} %broadcast_in_dim.12), calls=%async_computation.4 | async-start | bytes 4194304 | tf_op jit(solution)/shard_map/all_to_all | solution.py:36
  75.7 0.6 all-reduce.3.cloned.1.call-start
  76.6 47.6 %all-to-all-done.4 = f32[8,256,256]{2,1,0:T(8,128)} async-done(((f32[8,256,256]{2,1,0:T(8,128)}), f32[8,256,256]{2,1,0:T(8,128)}, u32[]{:S(2)}, u32[]{:S(2)}) %all-to-all-start.4) | async-done | bytes 2097184 | tf_op jit(solution)/shard_map/all_to_all | solution.py:36
  124.2 1.8 reduce_sum.47
  126.3 11.7 %cholesky.130 = f32[128,128]{1,0:T(8,128)S(1)} custom-call(f32[128,128]{1,0:T(8,128)S(1)} %cholesky.194), custom_call_target="Cholesky" | custom-call | tf_op jit(solution)/shard_map/jit(cholesky)/cholesky | solution.py:70
  138.1 9.8 %custom-call.17 = f32[1,128,128]{1,2,0:T(8,128)S(1)} custom-call(f32[1,128,128]{2,1,0:T(8,128)S(1)} %get-tuple-element.48), custom_call_target="InvertDiagBlocksLowerTriangular" | custom-call | tf_op jit(solution)/shard_map/jit(cholesky)/cholesky | solution.py:70
  148.4 11.7 %cholesky.147 = f32[128,128]{1,0:T(8,128)S(1)} custom-call(f32[128,128]{1,0:T(8,128)S(1)} %convolution_subtract_fusion.3), custom_call_target="Cholesky" | custom-call | tf_op jit(solution)/shard_map/jit(cholesky)/cholesky | solution.py:70
  160.1 0.7 compare_reduce_fusion.2
  162.2 4.2 %while.2 = (s32[]{:T(128)}, f32[256,256]{1,0:T(8,128)S(1)}, s32[2,2]{1,0:T(2,128)S(1)}, f32[2,128,128]{2,1,0:T(8,128)S(1)}, s32[]{:T(128)}) while((s32[]{:T(128)}, f32[256,256]{1,0:T(8,128)S(1)}, s32[2,2]{1,0:T(2,128)S(1)}, f32[2,128,128]{2,1,0:T(8,128)S(1)}, s32[]{:T(128)}) %tuple.48), condition=%wide.while_cond, body=%wide.while_body.sunk | while | flops 2 | bytes 131189 | solution.py:71
  162.4 0.7 fusion.41
  163.1 1.3 bitcast_dynamic-update-slice_fusion.4
  164.5 0.7 fusion.41
  165.1 1.3 bitcast_dynamic-update-slice_fusion.4
  166.5 19.7 %custom-call.14 = f32[2,128,128]{1,2,0:T(8,128)S(1)} custom-call(f32[2,128,128]{2,1,0:T(8,128)S(1)} %get-tuple-element.10), custom_call_target="InvertDiagBlocksLowerTriangular" | custom-call | tf_op jit(solution)/shard_map/triangular_solve | solution.py:71
  187.4 2.0 fusion.20
  189.5 77.3 %all-reduce.3.cloned.1.call-done = f32[256,2004]{0,1:T(8,128)} async-done(((f32[256,2004]{0,1:T(8,128)}), f32[256,2004]{0,1:T(8,128)}) %all-reduce.3.cloned.1.call-update) | async-done | bytes 2052112 | tf_op jit(solution)/shard_map/psum | solution.py:87
  266.8 5.7 %fusion.21 = f32[256,256]{1,0:T(8,128)S(1)} fusion(f32[256,2004]{0,1:T(8,128)} %all-reduce.3.cloned.1.call-done), kind=kOutput, calls=%fused_computation.63 | convolution fusion | flops 1576009728 | bytes 2314240 | tf_op jit(solution)/shard_map/dot_general | solution.py:66
  272.6 7.7 %all_to_all.47 = f32[2,32,4,256]{3,2,1,0:T(4,128)S(1)} all-to-all(f32[2,32,4,256]{3,2,1,0:T(4,128)S(1)} %bitcast.86), channel_id=1, replica_groups=mesh['row'=8,'col_0'=8,'col_1'=4,'col_2'=2] {'col_2'}, dimensions={0} | all-to-all | bytes 524288 | tf_op jit(solution)/shard_map/all_to_all | solution.py:17
  280.3 19.1 %all_to_all.50 = f32[32,4,256]{2,1,0:T(4,128)S(1)} all-to-all(f32[32,4,256]{2,1,0:T(4,128)S(1)} %reduce_sum.48), channel_id=1, replica_groups=mesh['row'=8,'col_0'=8,'col_1'=4,'col_2'=2] {'col_0','col_1'}, dimensions={0} | all-to-all | bytes 262144 | tf_op jit(solution)/shard_map/all_to_all | solution.py:25
  299.4 13.0 %all_to_all.51 = f32[32,4,256]{2,1,0:T(4,128)S(1)} all-to-all(f32[32,4,256]{2,1,0:T(4,128)S(1)} %broadcast_in_dim.14), channel_id=1, replica_groups=mesh['row'=8,'col_0'=8,'col_1'=4,'col_2'=2] {'col_0','col_1'}, dimensions={0} | all-to-all | bytes 262144 | tf_op jit(solution)/shard_map/all_to_all | solution.py:36
  312.5 6.7 %all_to_all.48 = f32[2,32,4,256]{3,2,1,0:T(4,128)S(1)} all-to-all(f32[2,32,4,256]{3,2,1,0:T(4,128)S(1)} %broadcast_in_dim.15), channel_id=1, replica_groups=mesh['row'=8,'col_0'=8,'col_1'=4,'col_2'=2] {'col_2'}, dimensions={0} | all-to-all | bytes 524288 | tf_op jit(solution)/shard_map/all_to_all | solution.py:36
  319.5 11.7 %cholesky.164 = f32[128,128]{1,0:T(8,128)S(1)} custom-call(f32[128,128]{1,0:T(8,128)S(1)} %cholesky.197), custom_call_target="Cholesky" | custom-call | tf_op jit(solution)/shard_map/jit(cholesky)/cholesky | solution.py:70
  331.3 0.7 compare_reduce_fusion.1
  332.0 9.8 %custom-call.18 = f32[1,128,128]{1,2,0:T(8,128)S(1)} custom-call(f32[1,128,128]{2,1,0:T(8,128)S(1)} %get-tuple-element.44), custom_call_target="InvertDiagBlocksLowerTriangular" | custom-call | tf_op jit(solution)/shard_map/jit(cholesky)/cholesky | solution.py:70
  342.3 11.7 %cholesky.181 = f32[128,128]{1,0:T(8,128)S(1)} custom-call(f32[128,128]{1,0:T(8,128)S(1)} %convolution_subtract_fusion.2), custom_call_target="Cholesky" | custom-call | tf_op jit(solution)/shard_map/jit(cholesky)/cholesky | solution.py:70
  354.1 0.6 compare_reduce_fusion
  356.0 4.1 %while.3 = (s32[]{:T(128)}, f32[256,256]{1,0:T(8,128)S(1)}, s32[2,2]{1,0:T(2,128)S(1)}, f32[2,128,128]{2,1,0:T(8,128)S(1)}, s32[]{:T(128)}) while((s32[]{:T(128)}, f32[256,256]{1,0:T(8,128)S(1)}, s32[2,2]{1,0:T(2,128)S(1)}, f32[2,128,128]{2,1,0:T(8,128)S(1)}, s32[]{:T(128)}) %tuple.56), condition=%wide.while_cond.1, body=%wide.while_body.1.sunk | while | flops 2 | bytes 131189 | solution.py:71
  356.0 0.7 fusion.42
  356.7 1.3 bitcast_dynamic-update-slice_fusion.5
  358.1 0.7 fusion.42
  358.7 1.3 bitcast_dynamic-update-slice_fusion.5
  360.1 19.9 %custom-call.15 = f32[2,128,128]{1,2,0:T(8,128)S(1)} custom-call(f32[2,128,128]{2,1,0:T(8,128)S(1)} %get-tuple-element.18), custom_call_target="InvertDiagBlocksLowerTriangular" | custom-call | tf_op jit(solution)/shard_map/triangular_solve | solution.py:71
  380.0 3.1 fusion.17
  383.2 1.8 convolution_subtract_fusion
  385.0 1.7 convolution_convert_fusion
  386.7 1.1 pad_maximum_fusion
  (57 shorter events, 4.3 us)
Async XLA Ops:
  7.2 1.6 copy-start
  11.7 11.7 %all-to-all-start = ((f32[2,32,4,512]{3,2,1,0:T(4,128)}), f32[2,32,4,512]{3,2,1,0:T(4,128)S(1)}, u32[]{:S(2)}, u32[]{:S(2)}) async-start(f32[2,32,4,512]{3,2,1,0:T(4,128)} %bitcast.70), calls=%async_computation | async-start | bytes 1048576 | tf_op jit(solution)/shard_map/all_to_all | solution.py:17
  68.9 55.3 %all-to-all-start.4 = ((f32[8,256,256]{2,1,0:T(8,128)}), f32[8,256,256]{2,1,0:T(8,128)}, u32[]{:S(2)}, u32[]{:S(2)}) async-start(f32[8,256,256]{2,1,0:T(8,128)} %broadcast_in_dim.12), calls=%async_computation.4 | async-start | bytes 4194304 | tf_op jit(solution)/shard_map/all_to_all | solution.py:36
  75.7 191.0 %all-reduce.3.cloned.1.call-start = ((), (), s32[]{:S(2)}) async-start(), calls=%async_computation.9 | async-start | bytes 4112384 | tf_op jit(solution)/shard_map/psum | solution.py:87
  187.4 2.0 copy-start.2
  380.0 3.1 copy-start.1
Sparse Core Ops, SparseCore 0:
  189.6 77.1 all-reduce.2
where the time goes:
time: 399 us; the launch traced here: 395 us
  waiting for transfers between devices  126 us (32%)
  other arithmetic  112 us (28%)
  blocking collectives  87.4 us (22%)
  matrix products  19.1 us (5%)
  starting transfers between devices  17.7 us (4%)
  between operations  17.2 us (4%)
  local copies, waits for them, and re-layouts  15.3 us (4%)
    psum x1, waiting for transfers between devices, local(): z_total = lax.psum(z_part, 'row')  77.3 us
    another operation x13, other arithmetic, solve_rows(): lower = jnp.linalg.cholesky(gram)  68.7 us
    all_to_all x1, waiting for transfers between devices, copy_for_each(): lax.all_to_all(jnp.broadcast_to(array[None], (peers, *array.shape)), axis...  47.6 us
    all_to_all x4, blocking collectives, copy_for_each(): lax.all_to_all(jnp.broadcast_to(array[None], (peers, *array.shape)), axis...  41.8 us
    another operation x7, other arithmetic, solve_rows(): lax.linalg.triangular_solve(lower, block, left_side=True, lower=True)  40.8 us
    all_to_all x2, blocking collectives, summed_rows(): lax.all_to_all(nearer, far, split_axis=0, concat_axis=0, tiled=True)  37.9 us
    all_to_all x1, starting transfers between devices, sum_at_owner(): lax.all_to_all(in_blocks(array, dim, peers), axis, 0, 0, tiled=True)  10.4 us
    another operation x12, local copies, waits for them, and re-layouts  8.04 us
  transfers between devices with their start and end apart: 3, of which 3 were waited for; matrix products, arithmetic and copies ran while one was open for 0% of the time, Pallas kernels for 0%

commit v1 on v0

v1 whole, which is shorter than its diff:
```python
import functools

import jax
import jax.numpy as jnp
from jax import lax
from jax.experimental import pallas as pl
from jax.experimental.pallas import tpu as pltpu
from jax.sharding import Mesh
from jax.sharding import PartitionSpec as P

F32 = jnp.float32
BF16 = jnp.bfloat16
MESH = pl.DeviceIdType.MESH
NY, NZ, NX, NK = 8, 8, 4, 2
SIZES = {"row": NY, "z": NZ, "x": NX, "k": NK}
VMEM = pl.BlockSpec(memory_space=pltpu.VMEM)
LIMIT = 56 << 20


def peer(axis, step):
    return lax.rem(lax.axis_index(axis) + (step + SIZES[axis]), SIZES[axis])


def greet(axes):
    barrier = pltpu.get_barrier_semaphore()
    count = 0
    for axis in axes:
        for step in range(1, SIZES[axis]):
            pl.semaphore_signal(barrier, inc=1, device_id={axis: peer(axis, step)}, device_id_type=MESH)
            count += 1
    return lambda: pl.semaphore_wait(barrier, count)


class Exchange:
    def __init__(self, axis, source, target, send, recv):
        self.copies = []
        for step in range(1, SIZES[axis]):
            to = peer(axis, step)
            self.copies.append(
                pltpu.make_async_remote_copy(
                    src_ref=source(to),
                    dst_ref=target(step),
                    send_sem=send.at[step - 1],
                    recv_sem=recv.at[step - 1],
                    device_id={axis: to},
                    device_id_type=MESH,
                )
            )
        for copy in self.copies:
            copy.start()

    def arrived(self):
        for copy in self.copies:
            copy.wait_recv()

    def sent(self):
        for copy in self.copies:
            copy.wait_send()


def part(index, size):
    return pl.ds(pl.multiple_of(index * size, size), size)


def tile_of(ref, index, width):
    return ref.at[..., part(index // 2, 8), part(lax.rem(index, 2), width)]


def dot(a, b, dims, precision=None):
    return lax.dot_general(a, b, (dims, ((), ())), precision=precision, preferred_element_type=F32)


def y_kernel(b_ref, p_ref, y_ref, away, home, from_k, from_x, strip, from_z, tile, sends, recvs):
    z, x, k = (lax.axis_index(a) for a in ("z", "x", "k"))
    wait_barrier = greet(("z", "x", "k"))
    away[...] = dot(b_ref[part(1 - k, 128), :], p_ref[...], ((1,), (1,)))
    wait_barrier()
    ex_k = Exchange("k", lambda to: away, lambda step: from_k, sends.at[0], recvs.at[0])
    own = dot(b_ref[part(k, 128), :], p_ref[...], ((1,), (1,)))
    ex_k.arrived()
    home[...] = own + from_k[...]
    ex_x = Exchange("x", lambda to: home.at[part(to, 32)], lambda step: from_x.at[step - 1], sends.at[1], recvs.at[1])
    ex_x.arrived()
    strip[...] = home[part(x, 32), :] + from_x[0] + from_x[1] + from_x[2]
    ex_z = Exchange("z", lambda to: tile_of(strip, to, 256), lambda step: from_z.at[step - 1], sends.at[2], recvs.at[2])
    ex_z.arrived()
    total = strip[part(z // 2, 8), part(lax.rem(z, 2), 256)]
    for step in range(NZ - 1):
        total += from_z[step]
    tile[...] = total
    half = y_ref.at[part(k, 128)]
    rows = half.at[part(x, 32)]
    tile_of(rows, z, 256)[...] = total
    ag_z = Exchange("z", lambda to: tile, lambda step: tile_of(rows, z, 256), sends.at[3], recvs.at[3])
    ag_z.arrived()
    ag_x = Exchange("x", lambda to: rows, lambda step: rows, sends.at[4], recvs.at[4])
    ag_x.arrived()
    ag_k = Exchange("k", lambda to: half, lambda step: half, sends.at[5], recvs.at[5])
    ag_k.arrived()
    for ex in (ex_k, ex_x, ex_z, ag_z, ag_x, ag_k):
        ex.sent()


def hop(axis, step, source, target, send, recv):
    copy = pltpu.make_async_remote_copy(
        src_ref=source,
        dst_ref=target,
        send_sem=send,
        recv_sem=recv,
        device_id={axis: peer(axis, step)},
        device_id_type=MESH,
    )
    copy.start()
    return copy


def w_kernel(rows_total, cols_total, y_ref, p_ref, g_ref, w_ref, parts, ring, gram, gram1, from_k, home, from_x, strip, from_z,
             tile, from_y, piece, rs_send, rs_recv, ag_send, ag_recv, sends, recvs):
    row, z, x, k = (lax.axis_index(a) for a in ("row", "z", "x", "k"))
    cols = p_ref.shape[1]
    wait_barrier = greet(("row", "z", "x", "k"))
    y = y_ref[...]
    high = y.astype(BF16)
    low = (y - high.astype(F32)).astype(BF16)
    for chunk in range(NY):
        width = min(256, cols - 256 * chunk)
        block = p_ref[:, 256 * chunk : 256 * chunk + width]
        value = dot(high, block, ((1,), (0,))) + dot(low, block, ((1,), (0,)))
        if width < 256:
            parts[chunk] = jnp.zeros((256, 256), F32)
        parts[chunk, :, :width] = value
    wait_barrier()
    waiting = []
    ways = (1, -1)
    sub = 2
    size = 128 // sub

    def lines(way, piece_no):
        return pl.ds((0 if way == 1 else 128) + piece_no * size, size)

    for step in range(NY - 1):
        for piece_no in range(sub):
            for w, way in enumerate(ways):
                at = lines(way, piece_no)
                if step:
                    flight[w, piece_no].wait_recv()
                    ring[step - 1, at, :] += parts[peer("row", -way * (step + 1)), at, :]
                    source = ring.at[step - 1, at]
                else:
                    source = parts.at[peer("row", -way), at]
                    flight = {} if (piece_no == 0 and w == 0) else flight
                copy = hop("row", way, source, ring.at[step, at], rs_send.at[step, w, piece_no], rs_recv.at[step, w, piece_no])
                waiting.append(copy)
                flight[w, piece_no] = copy
    gram1[...] = dot(y, y, ((1,), (1,)), lax.Precision.HIGHEST) / rows_total
    for piece_no in range(sub):
        for w, way in enumerate(ways):
            at = lines(way, piece_no)
            flight[w, piece_no].wait_recv()
            w_ref[row, at, :] = ring[NY - 2, at, :] + parts[row, at, :]
    mine = w_ref[row]
    gram[...] = dot(mine, mine, ((1,), (1,)), lax.Precision.HIGHEST)
    passed = {}

    def pass_on(step):
        for w, way in enumerate(ways):
            at = pl.ds(128 * w, 128)
            if step:
                passed[w].wait_recv()
            if step < NY - 1:
                block = w_ref.at[peer("row", -way * step), at]
                passed[w] = hop("row", way, block, block, ag_send.at[step, w], ag_recv.at[step, w])
                waiting.append(passed[w])

    ex = [Exchange("k", lambda to: gram.at[part(to, 128)], lambda step: from_k, sends.at[0], recvs.at[0])]
    pass_on(0)
    ex[-1].arrived()
    home[...] = gram[part(k, 128), :] + from_k[...]
    ex.append(Exchange("x", lambda to: home.at[part(to, 32)], lambda step: from_x.at[step - 1], sends.at[1], recvs.at[1]))
    pass_on(1)
    ex[-1].arrived()
    strip[...] = home[part(x, 32), :] + from_x[0] + from_x[1] + from_x[2]
    ex.append(Exchange("z", lambda to: tile_of(strip, to, 128), lambda step: from_z.at[step - 1], sends.at[2], recvs.at[2]))
    pass_on(2)
    ex[-1].arrived()
    total = strip[part(z // 2, 8), part(lax.rem(z, 2), 128)]
    for step in range(NZ - 1):
        total += from_z[step]
    tile[0] = gram1[pl.ds(pl.multiple_of(128 * k + 32 * x + 8 * (z // 2), 8), 8), part(lax.rem(z, 2), 128)]
    tile[1] = total
    ex.append(Exchange("row", lambda to: tile, lambda step: from_y.at[step - 1], sends.at[3], recvs.at[3]))
    pass_on(3)
    ex[-1].arrived()
    whole = tile[...]
    for step in range(NY - 1):
        whole += from_y[step]
    whole = jnp.stack([whole[0], whole[1] / cols_total])
    piece[...] = whole
    half = g_ref.at[:, part(k, 128)]
    rows = half.at[:, part(x, 32)]
    tile_of(rows, z, 128)[...] = whole
    ex.append(Exchange("z", lambda to: piece, lambda step: tile_of(rows, z, 128), sends.at[4], recvs.at[4]))
    pass_on(4)
    ex[-1].arrived()
    ex.append(Exchange("x", lambda to: rows, lambda step: rows, sends.at[5], recvs.at[5]))
    pass_on(5)
    ex[-1].arrived()
    ex.append(Exchange("k", lambda to: half, lambda step: half, sends.at[6], recvs.at[6]))
    pass_on(6)
    ex[-1].arrived()
    pass_on(7)
    for e in ex:
        e.sent()
    for copy in waiting:
        copy.wait_send()


def in_three(value):
    high = value.astype(BF16).astype(F32)
    rest = value - high
    middle = rest.astype(BF16).astype(F32)
    return high, middle, rest - middle


def spread_pair(a, b):
    h, m, l = in_three(a)
    i, n, o = in_three(b)
    return jnp.concatenate([h, h, m, h, l, m], 0).astype(BF16), jnp.concatenate([i, n, i, o, i, n], 0).astype(BF16)


def eliminate(block, base, count):
    size = block.shape[1]
    lane = lax.broadcasted_iota(jnp.int32, (1, size), 1)
    line = lax.broadcasted_iota(jnp.int32, (count, 1), 0)
    for i in range(count):
        unit = lane == base + i
        root = lax.rsqrt(block[i : i + 1, base + i : base + i + 1])
        row = jnp.where(unit, root, block[i : i + 1, :] * root)
        weight = jnp.where(line > i, block[:, base + i : base + i + 1] * root, 0.0)
        cleared = jnp.where(unit & (line > i), 0.0, block)
        block = jnp.where(line == i, row, cleared - weight * row)
    return block


def finish_kernel(g_ref, y_ref, w_ref, left_ref, right_ref, work, inverse):
    size, count = 256, 32
    work[...] = g_ref[...]
    lane = lax.broadcasted_iota(jnp.int32, (1, size), 1)
    line = lax.broadcasted_iota(jnp.int32, (count, 1), 0)
    for base in range(0, size, count):
        below = base + count
        for q in range(2):
            block = eliminate(work[q, base:below, :], base, count)
            lower = lane <= line + base
            inverse[q, base:below, :] = jnp.where(lower, block, 0.0)
            if below < size:
                a, b = spread_pair(block, jnp.where(lower | (lane >= below), block, 0.0))
                change = dot(a, b, ((0,), (0,)))[below:]
                panel = (lane >= base) & (lane < below)
                work[q, below:, :] = jnp.where(panel, 0.0, work[q, below:, :]) - change
    left_ref[...] = dot(inverse[0], y_ref[...], ((1,), (0,)), lax.Precision.HIGHEST).astype(BF16)
    cols = right_ref.shape[1]
    for chunk in range(NY):
        width = min(256, cols - 256 * chunk)
        value = dot(inverse[1], w_ref[chunk], ((1,), (0,)), lax.Precision.HIGHEST).astype(BF16)
        right_ref[:, 256 * chunk : 256 * chunk + width] = value[:, :width]


def local(ppmi, basis):
    rows, cols = ppmi.shape
    rows_total, cols_total = rows * NY, cols * NZ * NX * NK
    dma = pltpu.SemaphoreType.DMA
    params = functools.partial(pltpu.CompilerParams, has_side_effects=True, vmem_limit_bytes=LIMIT)
    y = pl.pallas_call(
        y_kernel,
        out_shape=jax.ShapeDtypeStruct((256, 512), F32),
        in_specs=[VMEM] * 2,
        out_specs=VMEM,
        scratch_shapes=[
            pltpu.VMEM((128, 512), F32),
            pltpu.VMEM((128, 512), F32),
            pltpu.VMEM((128, 512), F32),
            pltpu.VMEM((3, 32, 512), F32),
            pltpu.VMEM((32, 512), F32),
            pltpu.VMEM((7, 8, 256), F32),
            pltpu.VMEM((8, 256), F32),
            dma((6, 7)),
            dma((6, 7)),
        ],
        compiler_params=params(collective_id=0),
    )(basis, ppmi)
    gram, w = pl.pallas_call(
        functools.partial(w_kernel, rows_total, cols_total),
        out_shape=[jax.ShapeDtypeStruct((2, 256, 256), F32), jax.ShapeDtypeStruct((8, 256, 256), F32)],
        in_specs=[VMEM] * 2,
        out_specs=[VMEM] * 2,
        scratch_shapes=[
            pltpu.VMEM((8, 256, 256), F32),
            pltpu.VMEM((7, 256, 256), F32),
            pltpu.VMEM((256, 256), F32),
            pltpu.VMEM((256, 256), F32),
            pltpu.VMEM((128, 256), F32),
            pltpu.VMEM((128, 256), F32),
            pltpu.VMEM((3, 32, 256), F32),
            pltpu.VMEM((32, 256), F32),
            pltpu.VMEM((7, 8, 128), F32),
            pltpu.VMEM((2, 8, 128), F32),
            pltpu.VMEM((7, 2, 8, 128), F32),
            pltpu.VMEM((2, 8, 128), F32),
            dma((7, 2, 2)),
            dma((7, 2, 2)),
            dma((7, 2)),
            dma((7, 2)),
            dma((7, 7)),
            dma((7, 7)),
        ],
        compiler_params=params(collective_id=1),
    )(y, ppmi)
    return pl.pallas_call(
        finish_kernel,
        out_shape=[jax.ShapeDtypeStruct((256, rows), BF16), jax.ShapeDtypeStruct((256, cols), BF16)],
        in_specs=[VMEM] * 3,
        out_specs=[VMEM] * 2,
        scratch_shapes=[pltpu.VMEM((2, 256, 256), F32), pltpu.VMEM((2, 256, 256), F32)],
        compiler_params=pltpu.CompilerParams(vmem_limit_bytes=LIMIT),
    )(gram, y, w)


def solution(mesh):
    split = Mesh(mesh.devices.reshape(NY, NZ, NX, NK), ("row", "z", "x", "k"))
    col = ("z", "x", "k")
    return jax.shard_map(
        local,
        mesh=split,
        in_specs=(P("row", col), P(None, col)),
        out_specs=(P(None, "row"), P(None, col)),
        check_vma=False,
    )
```

time: 399 us -> 149 us (0.37)
  Pallas kernels: 0 us -> 138 us
  waiting for transfers between devices: 126 us -> 0 us
  other arithmetic: 112 us -> 0 us
  blocking collectives: 87.4 us -> 0 us
  matrix products: 19.1 us -> 0 us
  starting transfers between devices: 17.7 us -> 0 us
  between operations: 17.2 us -> 0.66 us
  local copies, waits for them, and re-layouts: 15.3 us -> 7.21 us
    pallas_call x0 -> x3, Pallas kernels: none -> 138 us  [the longest x1 70.1 us: local(): pl.pallas_call(functools.partial(w_kernel, rows_total, cols_total), out_s...]
    another operation x20 -> x0, other arithmetic: 109 us -> none  [the longest x13 68.7 us: solve_rows(): lower = jnp.linalg.cholesky(gram)]
    all_to_all x7 -> x0, blocking collectives: 87.4 us -> none  [the longest x4 41.8 us: copy_for_each(): lax.all_to_all(jnp.broadcast_to(array[None], (peers, *array.shape)), axis...]
    psum x1 -> x0, waiting for transfers between devices: 77.3 us -> none  [local(): z_total = lax.psum(z_part, 'row')]
    all_to_all x2 -> x0, waiting for transfers between devices: 48.9 us -> none  [the longest x1 47.6 us: copy_for_each(): lax.all_to_all(jnp.broadcast_to(array[None], (peers, *array.shape)), axis...]
    all_to_all x2 -> x0, starting transfers between devices: 17.2 us -> none  [the longest x1 10.4 us: sum_at_owner(): lax.all_to_all(in_blocks(array, dim, peers), axis, 0, 0, tiled=True)]
    another operation x27 -> x0, local copies, waits for them, and re-layouts: 10.7 us -> none
    dot_general x4 -> x0, matrix products: 10.2 us -> none  [the longest x2 6.29 us: local_gram(): return jnp.dot(block, block.T, precision=lax.Precision.HIGHEST)]
  transfers between devices with their start and end apart: 3 -> 0, of which waited for: 3 -> 0; matrix products, arithmetic and copies ran while one was open for 0% -> 0% of each run, Pallas kernels for 0% -> 0%
where the time goes in v1:
time: 149 us; the launch traced here: 146 us
  Pallas kernels  138 us (93%)
  local copies, waits for them, and re-layouts  7.21 us (5%)
    pallas_call x1, Pallas kernels, local(): pl.pallas_call(functools.partial(w_kernel, rows_total, cols_total), out_s...  70.1 us
    pallas_call x1, Pallas kernels, local(): pl.pallas_call(y_kernel, out_shape=jax.ShapeDtypeStruct((256, 512), F32),...  38.8 us
    pallas_call x1, Pallas kernels, local(): pl.pallas_call(finish_kernel, out_shape=[jax.ShapeDtypeStruct((256, rows)...  29.6 us
    unnamed x4, local copies, waits for them, and re-layouts  4.92 us

profile of v1, /device:TPU:1, one launch (start us, length us, event | category | flops | bytes accessed | tf_op | source)
XLA Modules:
  0.0 146.3 jit_solution(10157963018697839589)
XLA Ops:
  0.6 0.0 copy-start
  0.6 2.5 %copy.4.b_ref = bf16[256,2004]{1,0:T(8,128)(2,1)} copy(bf16[256,2004]{0,1:T(8,128)(2,1)} %param.3) | data formatting | bytes 2052096 | tf_op args[1]
  3.1 0.0 copy-done
  3.1 2.4 %copy.5.p_ref = bf16[512,2004]{1,0:T(8,128)(2,1)} copy(bf16[512,2004]{0,1:T(8,128)(2,1)S(1)} %copy-done) | data formatting | bytes 4104192 | tf_op args[0]
  5.6 38.8 %shard_map.41.y_ref = f32[256,512]{1,0:T(8,128)} custom-call(bf16[256,2004]{1,0:T(8,128)(2,1)} %copy.4.b_ref, bf16[512,2004]{1,0:T(8,128)(2,1)} %copy.5.p_ref), custom_call_target="tpu_custom_call" | custom-call | tf_op jit(solution)/shard_map/pallas_call | solution.py:274
  44.4 70.1 %shard_map.42 = (f32[2,256,256]{2,1,0:T(8,128)}, f32[8,256,256]{2,1,0:T(8,128)}) custom-call(f32[256,512]{1,0:T(8,128)} %shard_map.41.y_ref, bf16[512,2004]{1,0:T(8,128)(2,1)} %copy.5.p_ref), custom_call_target="tpu_custom_call" | custom-call | tf_op jit(solution)/shard_map/pallas_call | solution.py:292
  114.5 29.6 %shard_map.43 = (bf16[256,512]{1,0:T(8,128)(2,1)}, bf16[256,2004]{1,0:T(8,128)(2,1)}) custom-call(f32[2,256,256]{2,1,0:T(8,128)} %get-tuple-element.4.g_ref, f32[256,512]{1,0:T(8,128)} %shard_map.41.y_ref, f32[8,256,256]{2,1,0:T(8,128)} %get-tuple-element.5.w_ref), custom_call_target="tpu_custom_call" | custom-call | tf_op jit(solution)/shard_map/pallas_call | solution.py:319
  144.0 2.3 %copy.7 = bf16[256,2004]{0,1:T(8,128)(2,1)} copy(bf16[256,2004]{1,0:T(8,128)(2,1)} %get-tuple-element.7) | data formatting | bytes 2052096 | tf_op jit(solution)/shard_map/pallas_call | solution.py:319
Async XLA Ops:
  0.6 2.5 %copy-start = (bf16[512,2004]{0,1:T(8,128)(2,1)S(1)}, bf16[512,2004]{0,1:T(8,128)(2,1)}, u32[]{:S(2)}) copy-start(bf16[512,2004]{0,1:T(8,128)(2,1)} %param.2) | copy-start | bytes 6156292

commit v2 on v1

--- a/solution.py
+++ b/solution.py
@@ -73,10 +73,10 @@
 def y_kernel(b_ref, p_ref, y_ref, away, home, from_k, from_x, strip, from_z, tile, sends, recvs):
     z, x, k = (lax.axis_index(a) for a in ("z", "x", "k"))
     wait_barrier = greet(("z", "x", "k"))
-    away[...] = dot(b_ref[part(1 - k, 128), :], p_ref[...], ((1,), (1,)))
+    away[...] = dot(b_ref[:, part(1 - k, 128)], p_ref[...], ((0,), (0,)))
     wait_barrier()
     ex_k = Exchange("k", lambda to: away, lambda step: from_k, sends.at[0], recvs.at[0])
-    own = dot(b_ref[part(k, 128), :], p_ref[...], ((1,), (1,)))
+    own = dot(b_ref[:, part(k, 128)], p_ref[...], ((0,), (0,)))
     ex_k.arrived()
     home[...] = own + from_k[...]
     ex_x = Exchange("x", lambda to: home.at[part(to, 32)], lambda step: from_x.at[step - 1], sends.at[1], recvs.at[1])
@@ -117,18 +117,18 @@
 def w_kernel(rows_total, cols_total, y_ref, p_ref, g_ref, w_ref, parts, ring, gram, gram1, from_k, home, from_x, strip, from_z,
              tile, from_y, piece, rs_send, rs_recv, ag_send, ag_recv, sends, recvs):
     row, z, x, k = (lax.axis_index(a) for a in ("row", "z", "x", "k"))
-    cols = p_ref.shape[1]
+    cols = p_ref.shape[0]
     wait_barrier = greet(("row", "z", "x", "k"))
     y = y_ref[...]
     high = y.astype(BF16)
     low = (y - high.astype(F32)).astype(BF16)
     for chunk in range(NY):
         width = min(256, cols - 256 * chunk)
-        block = p_ref[:, 256 * chunk : 256 * chunk + width]
-        value = dot(high, block, ((1,), (0,))) + dot(low, block, ((1,), (0,)))
+        block = p_ref[256 * chunk : 256 * chunk + width, :]
+        value = dot(block, high, ((1,), (1,))) + dot(block, low, ((1,), (1,)))
         if width < 256:
-            parts[chunk] = jnp.zeros((256, 256), F32)
-        parts[chunk, :, :width] = value
+            parts[chunk, 128:, :] = jnp.zeros((128, 256), F32)
+        parts[chunk, :width, :] = value
     wait_barrier()
     waiting = []
     ways = (1, -1)
@@ -159,7 +159,7 @@
             flight[w, piece_no].wait_recv()
             w_ref[row, at, :] = ring[NY - 2, at, :] + parts[row, at, :]
     mine = w_ref[row]
-    gram[...] = dot(mine, mine, ((1,), (1,)), lax.Precision.HIGHEST)
+    gram[...] = dot(mine, mine, ((0,), (0,)), lax.Precision.HIGHEST)
     passed = {}
 
     def pass_on(step):
@@ -228,22 +228,72 @@
     return jnp.concatenate([h, h, m, h, l, m], 0).astype(BF16), jnp.concatenate([i, n, i, o, i, n], 0).astype(BF16)
 
 
+def spread(value):
+    return jnp.broadcast_to(value, (8, 128))
+
+
 def eliminate(block, base, count):
-    size = block.shape[1]
-    lane = lax.broadcasted_iota(jnp.int32, (1, size), 1)
-    line = lax.broadcasted_iota(jnp.int32, (count, 1), 0)
-    for i in range(count):
-        unit = lane == base + i
-        root = lax.rsqrt(block[i : i + 1, base + i : base + i + 1])
-        row = jnp.where(unit, root, block[i : i + 1, :] * root)
-        weight = jnp.where(line > i, block[:, base + i : base + i + 1] * root, 0.0)
-        cleared = jnp.where(unit & (line > i), 0.0, block)
-        block = jnp.where(line == i, row, cleared - weight * row)
-    return block
+    lane = lax.broadcasted_iota(jnp.int32, (8, 128), 1)
+    line = lax.broadcasted_iota(jnp.int32, (8, 128), 0)
+    groups = count // 8
+    tiles = [[block[8 * g : 8 * g + 8, 128 * h : 128 * h + 128] for g in range(groups)] for h in range(2)]
+    for now in range(groups):
+        side, first = divmod(base + 8 * now, 128)
+        rows = [[spread(tiles[h][now][a : a + 1, :]) for h in range(2)] for a in range(8)]
+        columns = [
+            {g: spread(tiles[side][g][:, first + a : first + a + 1]) for g in range(now, groups)} for a in range(8)
+        ]
+        corner = {(i, k): spread(columns[k][now][i : i + 1, :]) for i in range(8) for k in range(i + 1)}
+        factor, inverse = {}, {}
+        for a in range(8):
+            root = lax.rsqrt(corner[a, a])
+            inverse[a, a] = root
+            for i in range(a + 1, 8):
+                factor[i, a] = corner[i, a] * root
+            for i in range(a + 1, 8):
+                for k in range(a + 1, i + 1):
+                    corner[i, k] = corner[i, k] - factor[i, a] * factor[k, a]
+            for k in range(a):
+                total = factor[a, k] * inverse[k, k]
+                for q in range(k + 1, a):
+                    total = total + factor[a, q] * inverse[q, k]
+                inverse[a, k] = -(total * root)
+        done = []
+        for a in range(8):
+            pair = []
+            for h in range(2):
+                value = inverse[a, 0] * rows[0][h]
+                for k in range(1, a + 1):
+                    value = value + inverse[a, k] * rows[k][h]
+                if h == side:
+                    for k in range(8):
+                        value = jnp.where(lane == first + k, inverse[a, k] if k <= a else 0.0, value)
+                pair.append(value)
+            done.append(pair)
+        unit = (lane >= first) & (lane < first + 8)
+        for g in range(now + 1, groups):
+            weights = []
+            for a in range(8):
+                value = inverse[a, 0] * columns[0][g]
+                for k in range(1, a + 1):
+                    value = value + inverse[a, k] * columns[k][g]
+                weights.append(value)
+            for h in range(2):
+                change = weights[0] * done[0][h]
+                for a in range(1, 8):
+                    change = change + weights[a] * done[a][h]
+                old = jnp.where(unit, 0.0, tiles[h][g]) if h == side else tiles[h][g]
+                tiles[h][g] = old - change
+        for h in range(2):
+            value = done[0][h]
+            for a in range(1, 8):
+                value = jnp.where(line == a, done[a][h], value)
+            tiles[h][now] = value
+    return jnp.concatenate([jnp.concatenate(tiles[h], 0) for h in range(2)], 1)
 
 
 def finish_kernel(g_ref, y_ref, w_ref, left_ref, right_ref, work, inverse):
-    size, count = 256, 32
+    size, count = 256, 16
     work[...] = g_ref[...]
     lane = lax.broadcasted_iota(jnp.int32, (1, size), 1)
     line = lax.broadcasted_iota(jnp.int32, (count, 1), 0)
@@ -259,11 +309,11 @@
                 panel = (lane >= base) & (lane < below)
                 work[q, below:, :] = jnp.where(panel, 0.0, work[q, below:, :]) - change
     left_ref[...] = dot(inverse[0], y_ref[...], ((1,), (0,)), lax.Precision.HIGHEST).astype(BF16)
-    cols = right_ref.shape[1]
+    cols = right_ref.shape[0]
     for chunk in range(NY):
         width = min(256, cols - 256 * chunk)
-        value = dot(inverse[1], w_ref[chunk], ((1,), (0,)), lax.Precision.HIGHEST).astype(BF16)
-        right_ref[:, 256 * chunk : 256 * chunk + width] = value[:, :width]
+        value = dot(w_ref[chunk, :width], inverse[1], ((1,), (1,)), lax.Precision.HIGHEST)
+        right_ref[256 * chunk : 256 * chunk + width, :] = value.astype(BF16)
 
 
 def local(ppmi, basis):
@@ -288,7 +338,7 @@
             dma((6, 7)),
         ],
         compiler_params=params(collective_id=0),
-    )(basis, ppmi)
+    )(basis.T, ppmi.T)
     gram, w = pl.pallas_call(
         functools.partial(w_kernel, rows_total, cols_total),
         out_shape=[jax.ShapeDtypeStruct((2, 256, 256), F32), jax.ShapeDtypeStruct((8, 256, 256), F32)],
@@ -315,15 +365,16 @@
             dma((7, 7)),
         ],
         compiler_params=params(collective_id=1),
-    )(y, ppmi)
-    return pl.pallas_call(
+    )(y, ppmi.T)
+    left, right = pl.pallas_call(
         finish_kernel,
-        out_shape=[jax.ShapeDtypeStruct((256, rows), BF16), jax.ShapeDtypeStruct((256, cols), BF16)],
+        out_shape=[jax.ShapeDtypeStruct((256, rows), BF16), jax.ShapeDtypeStruct((cols, 256), BF16)],
         in_specs=[VMEM] * 3,
         out_specs=[VMEM] * 2,
         scratch_shapes=[pltpu.VMEM((2, 256, 256), F32), pltpu.VMEM((2, 256, 256), F32)],
         compiler_params=pltpu.CompilerParams(vmem_limit_bytes=LIMIT),
     )(gram, y, w)
+    return left, right.T
 
 
 def solution(mesh):

time: 149 us -> 131 us (0.88)
  the two profiles are of different devices: /device:TPU:1 before, /device:TPU:8 now
where the time goes in v2:
time: 131 us
  Pallas kernels  130 us (99%)
    pallas_call x1, Pallas kernels, local(): pl.pallas_call(functools.partial(w_kernel, rows_total, cols_total), out_s...  74.7 us
    pallas_call x1, Pallas kernels, local(): pl.pallas_call(y_kernel, out_shape=jax.ShapeDtypeStruct((256, 512), F32),...  37.1 us
    pallas_call x1, Pallas kernels, local(): pl.pallas_call(finish_kernel, out_shape=[jax.ShapeDtypeStruct((256, rows)...  18.1 us

profile of v2, /device:TPU:8, one launch (start us, length us, event | category | flops | bytes accessed | tf_op | source)
XLA Modules:
  0.0 130.5 jit_solution(5918451943036866226)
XLA Ops:
  0.6 37.1 %shard_map.41.y_ref = f32[256,512]{1,0:T(8,128)} custom-call(bf16[2004,256]{1,0:T(8,128)(2,1)} %bitcast.5, bf16[2004,512]{1,0:T(8,128)(2,1)} %bitcast.3), custom_call_target="tpu_custom_call" | custom-call | tf_op jit(solution)/shard_map/pallas_call | solution.py:324
  37.7 74.7 %shard_map.42 = (f32[2,256,256]{2,1,0:T(8,128)}, f32[8,256,256]{2,1,0:T(8,128)}) custom-call(f32[256,512]{1,0:T(8,128)} %shard_map.41.y_ref, bf16[2004,512]{1,0:T(8,128)(2,1)} %bitcast.4), custom_call_target="tpu_custom_call" | custom-call | tf_op jit(solution)/shard_map/pallas_call | solution.py:342
  112.4 18.1 %shard_map.43 = (bf16[256,512]{1,0:T(8,128)(2,1)}, bf16[2004,256]{1,0:T(8,128)(2,1)}) custom-call(f32[2,256,256]{2,1,0:T(8,128)} %get-tuple-element.6.g_ref, f32[256,512]{1,0:T(8,128)} %shard_map.41.y_ref, f32[8,256,256]{2,1,0:T(8,128)} %get-tuple-element.7.w_ref), custom_call_target="tpu_custom_call" | custom-call | tf_op jit(solution)/shard_map/pallas_call | solution.py:369

commit v3 on v2

v3 whole, which is shorter than its diff:
```python
import functools
import itertools

import jax
import jax.numpy as jnp
from jax import lax
from jax.experimental import pallas as pl
from jax.experimental.pallas import tpu as pltpu
from jax.sharding import Mesh
from jax.sharding import PartitionSpec as P

F32 = jnp.float32
BF16 = jnp.bfloat16
MESH = pl.DeviceIdType.MESH
NY, NZ, NX, NK = 8, 8, 4, 2
SIZES = {"row": NY, "z": NZ, "x": NX, "k": NK}
VMEM = pl.BlockSpec(memory_space=pltpu.VMEM)
LIMIT = 56 << 20


def peer(axis, step):
    return lax.rem(lax.axis_index(axis) + (step + SIZES[axis]), SIZES[axis])


def others(axes):
    steps = [step for step in itertools.product(*(range(SIZES[a]) for a in axes)) if any(step)]
    return sorted(steps, key=lambda step: -sum(min(s, SIZES[a] - s) for s, a in zip(step, axes)))


def greet(*groups):
    barrier = pltpu.get_barrier_semaphore()
    count = 0
    for axes in groups:
        for step in others(axes):
            to = {a: peer(a, s) for a, s in zip(axes, step)}
            pl.semaphore_signal(barrier, inc=1, device_id=to, device_id_type=MESH)
            count += 1
    return lambda: pl.semaphore_wait(barrier, count)


class Exchange:
    def __init__(self, axes, source, target, send, recv):
        self.copies = []
        for step in others(axes):
            to = {a: peer(a, s) for a, s in zip(axes, step)}
            number, slot = 0, 0
            for a, s in zip(axes, step):
                number, slot = number * SIZES[a] + to[a], slot * SIZES[a] + s
            self.copies.append(
                pltpu.make_async_remote_copy(
                    src_ref=source(number),
                    dst_ref=target(slot - 1),
                    send_sem=send.at[slot - 1],
                    recv_sem=recv.at[slot - 1],
                    device_id=to,
                    device_id_type=MESH,
                )
            )
        for copy in self.copies:
            copy.start()

    def arrived(self):
        for copy in self.copies:
            copy.wait_recv()

    def sent(self):
        for copy in self.copies:
            copy.wait_send()


def part(index, size):
    return pl.ds(pl.multiple_of(index * size, size), size)


def tile_of(ref, index, width):
    return ref.at[..., part(index // 2, 8), part(lax.rem(index, 2), width)]


def dot(a, b, dims, precision=None):
    return lax.dot_general(a, b, (dims, ((), ())), precision=precision, preferred_element_type=F32)


def y_kernel(b_ref, p_ref, y_ref, away, home, from_k, from_x, strip, from_z, tile, sends, recvs):
    z, x, k = (lax.axis_index(a) for a in "zxk")
    wait_barrier = greet("z", "x", "k")
    away[...] = dot(p_ref[:, part(1 - k, 256)], b_ref[...], ((0,), (0,)))
    wait_barrier()
    ex = [Exchange("k", lambda to: away, lambda slot: from_k, sends.at[0], recvs.at[0])]
    own = dot(p_ref[:, part(k, 256)], b_ref[...], ((0,), (0,)))
    ex[-1].arrived()
    home[...] = own + from_k[...]
    ex.append(Exchange("x", lambda to: home.at[part(to, 64)], lambda slot: from_x.at[slot], sends.at[1], recvs.at[1]))
    ex[-1].arrived()
    strip[...] = home[part(x, 64), :] + from_x[0] + from_x[1] + from_x[2]
    ex.append(Exchange("z", lambda to: strip.at[part(to, 8)], lambda slot: from_z.at[slot], sends.at[2], recvs.at[2]))
    ex[-1].arrived()
    total = strip[part(z, 8), :]
    for slot in range(NZ - 1):
        total += from_z[slot]
    tile[...] = total
    half = y_ref.at[part(k, 256)]
    rows = half.at[part(x, 64)]
    rows[part(z, 8), :] = total
    ex.append(Exchange("z", lambda to: tile, lambda slot: rows.at[part(z, 8)], sends.at[3], recvs.at[3]))
    ex[-1].arrived()
    ex.append(Exchange("x", lambda to: rows, lambda slot: rows, sends.at[4], recvs.at[4]))
    ex[-1].arrived()
    ex.append(Exchange("k", lambda to: half, lambda slot: half, sends.at[5], recvs.at[5]))
    for e in ex:
        e.sent()
    ex[-1].arrived()


def hop(axis, step, source, target, send, recv):
    copy = pltpu.make_async_remote_copy(
        src_ref=source,
        dst_ref=target,
        send_sem=send,
        recv_sem=recv,
        device_id={axis: peer(axis, step)},
        device_id_type=MESH,
    )
    copy.start()
    return copy


WAYS = (1, -1)


def chain(way, half):
    return 4 if (way == 1) == (half == 0) else 3


SPAN = 250.0


def encode(value, out):
    rows = value.shape[0]
    size = jnp.abs(value).reshape(rows // 8, 8, 256)
    scale = jnp.maximum(jnp.max(size, axis=0) * (1 + 2.0**-7), 1e-30).astype(BF16)
    power = jnp.exp2(size * (SPAN / scale.astype(F32)) - SPAN / 2).reshape(rows, 256)
    out[:rows, :] = jnp.where(value < 0, -power, power).astype(BF16)
    out[rows:, :] = jnp.concatenate([scale, scale], 0)


def decode(coded):
    rows = coded.shape[0] - 16
    value = coded[:rows, :].astype(F32)
    scale = coded[rows : rows + 8, :].astype(F32) * (1 / SPAN)
    size = (jnp.log2(jnp.abs(value)) + SPAN / 2).reshape(rows // 8, 8, 256) * scale
    size = size.reshape(rows, 256)
    return jnp.where(value < 0, -size, size)


class Ring:
    def __init__(self, parts, out, ring, send, recv):
        self.parts, self.out, self.ring, self.send, self.recv = parts, out, ring, send, recv
        self.flight, self.waiting = {}, []

    def step(self, step):
        for half in range(2):
            at = pl.ds(128 * half, 128)
            for w, way in enumerate(WAYS):
                hops = chain(way, half)
                if step >= hops:
                    continue
                total = self.parts[peer("row", way * (hops - step)), at, :]
                if step:
                    self.flight[w, half].wait_recv()
                    total += decode(self.ring[step - 1, w, half])
                encode(total, self.out.at[step, w, half])
                copy = hop(
                    "row",
                    way,
                    self.out.at[step, w, half],
                    self.ring.at[step, w, half],
                    self.send.at[step, w, half],
                    self.recv.at[step, w, half],
                )
                self.waiting.append(copy)
                self.flight[w, half] = copy

    def last(self, target):
        row = lax.axis_index("row")
        for half in range(2):
            at = pl.ds(128 * half, 128)
            total = self.parts[row, at, :]
            for w, way in enumerate(WAYS):
                self.flight[w, half].wait_recv()
                total += decode(self.ring[chain(way, half) - 1, w, half])
            target[at, :] = total


class Gather:
    def __init__(self, blocks, send, recv):
        self.blocks, self.send, self.recv = blocks, send, recv
        self.flight, self.waiting = {}, []

    def step(self, step):
        for half in range(2):
            for w, way in enumerate(WAYS):
                hops = chain(way, half)
                if 0 < step <= hops:
                    self.flight[w, half].wait_recv()
                if step < hops:
                    block = self.blocks.at[peer("row", -way * step), half]
                    copy = hop("row", way, block, block, self.send.at[step, w, half], self.recv.at[step, w, half])
                    self.waiting.append(copy)
                    self.flight[w, half] = copy


def w_kernel(rows_total, cols_total, y_ref, p_ref, g_ref, w_ref, parts, out, ring, mine, gram, gram1, from_k, home, from_zx, tile,
             from_y, piece, rs_send, rs_recv, ag_send, ag_recv, sends, recvs):
    row, k = lax.axis_index("row"), lax.axis_index("k")
    me = lax.axis_index("z") * NX + lax.axis_index("x")
    cols = p_ref.shape[0]
    wait_barrier = greet(("row",), "zx", "k")
    y = y_ref[...]
    high = y.astype(BF16)
    low = (y - high.astype(F32)).astype(BF16)
    for chunk in range(NY):
        width = min(256, cols - 256 * chunk)
        block = p_ref[256 * chunk : 256 * chunk + width, :]
        value = dot(block, high, ((1,), (0,))) + dot(block, low, ((1,), (0,)))
        if width < 256:
            parts[chunk, 128:, :] = jnp.zeros((128, 256), F32)
        parts[chunk, :width, :] = value
    wait_barrier()
    reduce = Ring(parts, out, ring, rs_send, rs_recv)
    for step in range(4):
        reduce.step(step)
    gram1[...] = dot(y, y, ((0,), (0,)), lax.Precision.HIGHEST) / rows_total
    reduce.last(mine)
    for half in range(2):
        encode(mine[pl.ds(128 * half, 128), :], w_ref.at[row, half])
    gram[...] = dot(mine[...], mine[...], ((0,), (0,)), lax.Precision.HIGHEST)
    gather = Gather(w_ref, ag_send, ag_recv)
    ex = [Exchange("k", lambda to: gram.at[part(to, 128)], lambda slot: from_k, sends.at[0], recvs.at[0])]
    gather.step(0)
    ex[-1].arrived()
    home[...] = gram[part(k, 128), :] + from_k[...]
    ex.append(Exchange("zx", lambda to: tile_of(home, to, 128), lambda slot: from_zx.at[slot], sends.at[1], recvs.at[1]))
    gather.step(1)
    ex[-1].arrived()
    total = tile_of(home, me, 128)[...]
    for slot in range(NZ * NX - 1):
        total += from_zx[slot]
    tile[0] = gram1[pl.ds(pl.multiple_of(128 * k + 8 * (me // 2), 8), 8), part(lax.rem(me, 2), 128)]
    tile[1] = total
    from_y[row] = tile[...]
    ex.append(Exchange(("row",), lambda to: tile, lambda slot: from_y.at[row], sends.at[2], recvs.at[2]))
    gather.step(2)
    ex[-1].arrived()
    whole = from_y[0]
    for slot in range(1, NY):
        whole += from_y[slot]
    whole = jnp.stack([whole[0], whole[1] / cols_total])
    piece[...] = whole
    half = g_ref.at[:, part(k, 128)]
    tile_of(half, me, 128)[...] = whole
    ex.append(Exchange("zx", lambda to: piece, lambda slot: tile_of(half, me, 128), sends.at[3], recvs.at[3]))
    gather.step(3)
    ex[-1].arrived()
    ex.append(Exchange("k", lambda to: half, lambda slot: half, sends.at[4], recvs.at[4]))
    gather.step(4)
    for e in ex:
        e.sent()
    ex[-1].arrived()
    for copy in reduce.waiting + gather.waiting:
        copy.wait_send()


def in_three(value):
    high = value.astype(BF16).astype(F32)
    rest = value - high
    middle = rest.astype(BF16).astype(F32)
    return high, middle, rest - middle


def spread_pair(a, b):
    h, m, l = in_three(a)
    i, n, o = in_three(b)
    return jnp.concatenate([h, h, m, h, l, m], 0).astype(BF16), jnp.concatenate([i, n, i, o, i, n], 0).astype(BF16)


def spread(value):
    return jnp.broadcast_to(value, (8, 128))


def eliminate(block, base, count):
    lane = lax.broadcasted_iota(jnp.int32, (8, 128), 1)
    line = lax.broadcasted_iota(jnp.int32, (8, 128), 0)
    groups = count // 8
    tiles = [[block[8 * g : 8 * g + 8, 128 * h : 128 * h + 128] for g in range(groups)] for h in range(2)]
    for now in range(groups):
        side, first = divmod(base + 8 * now, 128)
        rows = [[spread(tiles[h][now][a : a + 1, :]) for h in range(2)] for a in range(8)]
        columns = [
            {g: spread(tiles[side][g][:, first + a : first + a + 1]) for g in range(now, groups)} for a in range(8)
        ]
        corner = {(i, k): spread(columns[k][now][i : i + 1, :]) for i in range(8) for k in range(i + 1)}
        factor, inverse = {}, {}
        for a in range(8):
            root = lax.rsqrt(corner[a, a])
            inverse[a, a] = root
            for i in range(a + 1, 8):
                factor[i, a] = corner[i, a] * root
            for i in range(a + 1, 8):
                for k in range(a + 1, i + 1):
                    corner[i, k] = corner[i, k] - factor[i, a] * factor[k, a]
            for k in range(a):
                total = factor[a, k] * inverse[k, k]
                for q in range(k + 1, a):
                    total = total + factor[a, q] * inverse[q, k]
                inverse[a, k] = -(total * root)
        done = []
        for a in range(8):
            pair = []
            for h in range(2):
                value = inverse[a, 0] * rows[0][h]
                for k in range(1, a + 1):
                    value = value + inverse[a, k] * rows[k][h]
                if h == side:
                    for k in range(8):
                        value = jnp.where(lane == first + k, inverse[a, k] if k <= a else 0.0, value)
                pair.append(value)
            done.append(pair)
        unit = (lane >= first) & (lane < first + 8)
        for g in range(now + 1, groups):
            weights = []
            for a in range(8):
                value = inverse[a, 0] * columns[0][g]
                for k in range(1, a + 1):
                    value = value + inverse[a, k] * columns[k][g]
                weights.append(value)
            for h in range(2):
                change = weights[0] * done[0][h]
                for a in range(1, 8):
                    change = change + weights[a] * done[a][h]
                old = jnp.where(unit, 0.0, tiles[h][g]) if h == side else tiles[h][g]
                tiles[h][g] = old - change
        for h in range(2):
            value = done[0][h]
            for a in range(1, 8):
                value = jnp.where(line == a, done[a][h], value)
            tiles[h][now] = value
    return jnp.concatenate([jnp.concatenate(tiles[h], 0) for h in range(2)], 1)


def finish_kernel(g_ref, y_ref, w_ref, left_ref, right_ref, work, inverse):
    size, count = 256, 16
    work[...] = g_ref[...]
    lane = lax.broadcasted_iota(jnp.int32, (1, size), 1)
    line = lax.broadcasted_iota(jnp.int32, (count, 1), 0)
    for base in range(0, size, count):
        below = base + count
        for q in range(2):
            block = eliminate(work[q, base:below, :], base, count)
            lower = lane <= line + base
            inverse[q, base:below, :] = jnp.where(lower, block, 0.0)
            if below < size:
                a, b = spread_pair(block, jnp.where(lower | (lane >= below), block, 0.0))
                change = dot(a, b, ((0,), (0,)))[below:]
                panel = (lane >= base) & (lane < below)
                work[q, below:, :] = jnp.where(panel, 0.0, work[q, below:, :]) - change
    left_ref[...] = dot(inverse[0], y_ref[...], ((1,), (1,)), lax.Precision.HIGHEST).astype(BF16)
    cols = right_ref.shape[0]
    for chunk in range(2 * NY):
        width = min(128, cols - 128 * chunk)
        value = dot(decode(w_ref[chunk // 2, chunk % 2]), inverse[1], ((1,), (1,)), lax.Precision.HIGHEST)
        right_ref[128 * chunk : 128 * chunk + width, :] = value[:width].astype(BF16)


def local(ppmi, basis):
    rows, cols = ppmi.shape
    rows_total, cols_total = rows * NY, cols * NZ * NX * NK
    dma = pltpu.SemaphoreType.DMA
    params = functools.partial(pltpu.CompilerParams, has_side_effects=True, vmem_limit_bytes=LIMIT)
    y = pl.pallas_call(
        y_kernel,
        out_shape=jax.ShapeDtypeStruct((512, 256), F32),
        in_specs=[VMEM] * 2,
        out_specs=VMEM,
        scratch_shapes=[
            pltpu.VMEM((256, 256), F32),
            pltpu.VMEM((256, 256), F32),
            pltpu.VMEM((256, 256), F32),
            pltpu.VMEM((3, 64, 256), F32),
            pltpu.VMEM((64, 256), F32),
            pltpu.VMEM((7, 8, 256), F32),
            pltpu.VMEM((8, 256), F32),
            dma((6, 7)),
            dma((6, 7)),
        ],
        compiler_params=params(collective_id=0),
    )(basis.T, ppmi.T)
    gram, w = pl.pallas_call(
        functools.partial(w_kernel, rows_total, cols_total),
        out_shape=[jax.ShapeDtypeStruct((2, 256, 256), F32), jax.ShapeDtypeStruct((8, 2, 144, 256), BF16)],
        in_specs=[VMEM] * 2,
        out_specs=[VMEM] * 2,
        scratch_shapes=[
            pltpu.VMEM((8, 256, 256), F32),
            pltpu.VMEM((4, 2, 2, 144, 256), BF16),
            pltpu.VMEM((4, 2, 2, 144, 256), BF16),
            pltpu.VMEM((256, 256), F32),
            pltpu.VMEM((256, 256), F32),
            pltpu.VMEM((256, 256), F32),
            pltpu.VMEM((128, 256), F32),
            pltpu.VMEM((128, 256), F32),
            pltpu.VMEM((31, 8, 128), F32),
            pltpu.VMEM((2, 8, 128), F32),
            pltpu.VMEM((8, 2, 8, 128), F32),
            pltpu.VMEM((2, 8, 128), F32),
            dma((4, 2, 2)),
            dma((4, 2, 2)),
            dma((4, 2, 2)),
            dma((4, 2, 2)),
            dma((5, 31)),
            dma((5, 31)),
        ],
        compiler_params=params(collective_id=1),
    )(y, ppmi.T)
    left, right = pl.pallas_call(
        finish_kernel,
        out_shape=[jax.ShapeDtypeStruct((256, rows), BF16), jax.ShapeDtypeStruct((cols, 256), BF16)],
        in_specs=[VMEM] * 3,
        out_specs=[VMEM] * 2,
        scratch_shapes=[pltpu.VMEM((2, 256, 256), F32), pltpu.VMEM((2, 256, 256), F32)],
        compiler_params=pltpu.CompilerParams(vmem_limit_bytes=LIMIT),
    )(gram, y, w)
    return left, right.T


def solution(mesh):
    split = Mesh(mesh.devices.reshape(NY, NZ, NX, NK), ("row", "z", "x", "k"))
    col = ("z", "x", "k")
    return jax.shard_map(
        local,
        mesh=split,
        in_specs=(P("row", col), P(None, col)),
        out_specs=(P(None, "row"), P(None, col)),
        check_vma=False,
    )
```

time: 131 us -> 114 us (0.87)
  the two profiles are of different devices: /device:TPU:8 before, /device:TPU:1 now
where the time goes in v3:
time: 114 us
  Pallas kernels  113 us (99%)
    pallas_call x1, Pallas kernels, local(): pl.pallas_call(functools.partial(w_kernel, rows_total, cols_total), out_s...  55.2 us
    pallas_call x1, Pallas kernels, local(): pl.pallas_call(y_kernel, out_shape=jax.ShapeDtypeStruct((512, 256), F32),...  37.9 us
    pallas_call x1, Pallas kernels, local(): pl.pallas_call(finish_kernel, out_shape=[jax.ShapeDtypeStruct((256, rows)...  20.2 us

profile of v3, /device:TPU:1, one launch (start us, length us, event | category | flops | bytes accessed | tf_op | source)
XLA Modules:
  0.0 114.0 jit_solution(12674818060597086015)
XLA Ops:
  0.6 37.9 %shard_map.41.y_ref = f32[512,256]{1,0:T(8,128)} custom-call(bf16[2004,256]{1,0:T(8,128)(2,1)} %bitcast.5, bf16[2004,512]{1,0:T(8,128)(2,1)} %bitcast.3), custom_call_target="tpu_custom_call" | custom-call | tf_op jit(solution)/shard_map/pallas_call | solution.py:379
  38.6 55.2 %shard_map.42 = (f32[2,256,256]{2,1,0:T(8,128)}, bf16[8,2,144,256]{3,2,1,0:T(8,128)(2,1)}) custom-call(f32[512,256]{1,0:T(8,128)} %shard_map.41.y_ref, bf16[2004,512]{1,0:T(8,128)(2,1)} %bitcast.4), custom_call_target="tpu_custom_call" | custom-call | tf_op jit(solution)/shard_map/pallas_call | solution.py:397
  93.8 20.2 %shard_map.43 = (bf16[256,512]{1,0:T(8,128)(2,1)}, bf16[2004,256]{1,0:T(8,128)(2,1)}) custom-call(f32[2,256,256]{2,1,0:T(8,128)} %get-tuple-element.6.g_ref, f32[512,256]{1,0:T(8,128)} %shard_map.41.y_ref, bf16[8,2,144,256]{3,2,1,0:T(8,128)(2,1)} %get-tuple-element.7.w_ref), custom_call_target="tpu_custom_call" | custom-call | tf_op jit(solution)/shard_map/pallas_call | solution.py:424

commit v4 on v3

--- a/solution.py
+++ b/solution.py
@@ -80,35 +80,60 @@
     return lax.dot_general(a, b, (dims, ((), ())), precision=precision, preferred_element_type=F32)
 
 
-def y_kernel(b_ref, p_ref, y_ref, away, home, from_k, from_x, strip, from_z, tile, sends, recvs):
+SPAN = 250.0
+
+
+def encode(value, out):
+    rows = value.shape[0]
+    size = jnp.abs(value).reshape(rows // 8, 8, 256)
+    scale = jnp.maximum(jnp.max(size, axis=0) * (1 + 2.0**-7), 1e-30).astype(BF16)
+    power = jnp.exp2(size * (SPAN / scale.astype(F32)) - SPAN / 2).reshape(rows, 256)
+    out[:rows, :] = jnp.where(value < 0, -power, power).astype(BF16)
+    out[rows:, :] = jnp.concatenate([scale, scale], 0)
+
+
+def decode(coded):
+    rows = coded.shape[0] - 16
+    value = coded[:rows, :].astype(F32)
+    scale = coded[rows : rows + 8, :].astype(F32) * (1 / SPAN)
+    size = (jnp.log2(jnp.abs(value)) + SPAN / 2).reshape(rows // 8, 8, 256) * scale
+    size = size.reshape(rows, 256)
+    return jnp.where(value < 0, -size, size)
+
+
+def sum_y(wait_barrier, b_ref, p_ref, y_ref, away, home, from_k, out_x, from_x, strip, from_z, tile, rows, coded, sends, recvs):
     z, x, k = (lax.axis_index(a) for a in "zxk")
-    wait_barrier = greet("z", "x", "k")
     away[...] = dot(p_ref[:, part(1 - k, 256)], b_ref[...], ((0,), (0,)))
     wait_barrier()
     ex = [Exchange("k", lambda to: away, lambda slot: from_k, sends.at[0], recvs.at[0])]
     own = dot(p_ref[:, part(k, 256)], b_ref[...], ((0,), (0,)))
     ex[-1].arrived()
     home[...] = own + from_k[...]
-    ex.append(Exchange("x", lambda to: home.at[part(to, 64)], lambda slot: from_x.at[slot], sends.at[1], recvs.at[1]))
-    ex[-1].arrived()
-    strip[...] = home[part(x, 64), :] + from_x[0] + from_x[1] + from_x[2]
+    for number in range(NX):
+        encode(home[64 * number : 64 * number + 64, :], out_x.at[number])
+    ex.append(Exchange("x", lambda to: out_x.at[to], lambda slot: from_x.at[slot], sends.at[1], recvs.at[1]))
+    ex[-1].arrived()
+    total = home[part(x, 64), :]
+    for slot in range(NX - 1):
+        total += decode(from_x[slot])
+    strip[...] = total
     ex.append(Exchange("z", lambda to: strip.at[part(to, 8)], lambda slot: from_z.at[slot], sends.at[2], recvs.at[2]))
     ex[-1].arrived()
     total = strip[part(z, 8), :]
     for slot in range(NZ - 1):
         total += from_z[slot]
     tile[...] = total
-    half = y_ref.at[part(k, 256)]
-    rows = half.at[part(x, 64)]
     rows[part(z, 8), :] = total
     ex.append(Exchange("z", lambda to: tile, lambda slot: rows.at[part(z, 8)], sends.at[3], recvs.at[3]))
     ex[-1].arrived()
-    ex.append(Exchange("x", lambda to: rows, lambda slot: rows, sends.at[4], recvs.at[4]))
-    ex[-1].arrived()
-    ex.append(Exchange("k", lambda to: half, lambda slot: half, sends.at[5], recvs.at[5]))
-    for e in ex:
-        e.sent()
-    ex[-1].arrived()
+    encode(rows[...], coded.at[k, x])
+    ex.append(Exchange("x", lambda to: coded.at[k, x], lambda slot: coded.at[k, x], sends.at[4], recvs.at[4]))
+    ex[-1].arrived()
+    ex.append(Exchange("k", lambda to: coded.at[k], lambda slot: coded.at[k], sends.at[5], recvs.at[5]))
+    ex[-1].arrived()
+    for number in range(NK * NX):
+        y_ref[64 * number : 64 * number + 64, :] = decode(coded[number // NX, number % NX])
+    return ex
 
 
 def hop(axis, step, source, target, send, recv):
@@ -129,27 +154,6 @@
 
 def chain(way, half):
     return 4 if (way == 1) == (half == 0) else 3
-
-
-SPAN = 250.0
-
-
-def encode(value, out):
-    rows = value.shape[0]
-    size = jnp.abs(value).reshape(rows // 8, 8, 256)
-    scale = jnp.maximum(jnp.max(size, axis=0) * (1 + 2.0**-7), 1e-30).astype(BF16)
-    power = jnp.exp2(size * (SPAN / scale.astype(F32)) - SPAN / 2).reshape(rows, 256)
-    out[:rows, :] = jnp.where(value < 0, -power, power).astype(BF16)
-    out[rows:, :] = jnp.concatenate([scale, scale], 0)
-
-
-def decode(coded):
-    rows = coded.shape[0] - 16
-    value = coded[:rows, :].astype(F32)
-    scale = coded[rows : rows + 8, :].astype(F32) * (1 / SPAN)
-    size = (jnp.log2(jnp.abs(value)) + SPAN / 2).reshape(rows // 8, 8, 256) * scale
-    size = size.reshape(rows, 256)
-    return jnp.where(value < 0, -size, size)
 
 
 class Ring:
@@ -207,67 +211,6 @@
                     copy = hop("row", way, block, block, self.send.at[step, w, half], self.recv.at[step, w, half])
                     self.waiting.append(copy)
                     self.flight[w, half] = copy
-
-
-def w_kernel(rows_total, cols_total, y_ref, p_ref, g_ref, w_ref, parts, out, ring, mine, gram, gram1, from_k, home, from_zx, tile,
-             from_y, piece, rs_send, rs_recv, ag_send, ag_recv, sends, recvs):
-    row, k = lax.axis_index("row"), lax.axis_index("k")
-    me = lax.axis_index("z") * NX + lax.axis_index("x")
-    cols = p_ref.shape[0]
-    wait_barrier = greet(("row",), "zx", "k")
-    y = y_ref[...]
-    high = y.astype(BF16)
-    low = (y - high.astype(F32)).astype(BF16)
-    for chunk in range(NY):
-        width = min(256, cols - 256 * chunk)
-        block = p_ref[256 * chunk : 256 * chunk + width, :]
-        value = dot(block, high, ((1,), (0,))) + dot(block, low, ((1,), (0,)))
-        if width < 256:
-            parts[chunk, 128:, :] = jnp.zeros((128, 256), F32)
-        parts[chunk, :width, :] = value
-    wait_barrier()
-    reduce = Ring(parts, out, ring, rs_send, rs_recv)
-    for step in range(4):
-        reduce.step(step)
-    gram1[...] = dot(y, y, ((0,), (0,)), lax.Precision.HIGHEST) / rows_total
-    reduce.last(mine)
-    for half in range(2):
-        encode(mine[pl.ds(128 * half, 128), :], w_ref.at[row, half])
-    gram[...] = dot(mine[...], mine[...], ((0,), (0,)), lax.Precision.HIGHEST)
-    gather = Gather(w_ref, ag_send, ag_recv)
-    ex = [Exchange("k", lambda to: gram.at[part(to, 128)], lambda slot: from_k, sends.at[0], recvs.at[0])]
-    gather.step(0)
-    ex[-1].arrived()
-    home[...] = gram[part(k, 128), :] + from_k[...]
-    ex.append(Exchange("zx", lambda to: tile_of(home, to, 128), lambda slot: from_zx.at[slot], sends.at[1], recvs.at[1]))
-    gather.step(1)
-    ex[-1].arrived()
-    total = tile_of(home, me, 128)[...]
-    for slot in range(NZ * NX - 1):
-        total += from_zx[slot]
-    tile[0] = gram1[pl.ds(pl.multiple_of(128 * k + 8 * (me // 2), 8), 8), part(lax.rem(me, 2), 128)]
-    tile[1] = total
-    from_y[row] = tile[...]
-    ex.append(Exchange(("row",), lambda to: tile, lambda slot: from_y.at[row], sends.at[2], recvs.at[2]))
-    gather.step(2)
-    ex[-1].arrived()
-    whole = from_y[0]
-    for slot in range(1, NY):
-        whole += from_y[slot]
-    whole = jnp.stack([whole[0], whole[1] / cols_total])
-    piece[...] = whole
-    half = g_ref.at[:, part(k, 128)]
-    tile_of(half, me, 128)[...] = whole
-    ex.append(Exchange("zx", lambda to: piece, lambda slot: tile_of(half, me, 128), sends.at[3], recvs.at[3]))
-    gather.step(3)
-    ex[-1].arrived()
-    ex.append(Exchange("k", lambda to: half, lambda slot: half, sends.at[4], recvs.at[4]))
-    gather.step(4)
-    for e in ex:
-        e.sent()
-    ex[-1].arrived()
-    for copy in reduce.waiting + gather.waiting:
-        copy.wait_send()
 
 
 def in_three(value):
@@ -347,27 +290,138 @@
     return jnp.concatenate([jnp.concatenate(tiles[h], 0) for h in range(2)], 1)
 
 
-def finish_kernel(g_ref, y_ref, w_ref, left_ref, right_ref, work, inverse):
+def inverse_steps(work, inverse):
     size, count = 256, 16
-    work[...] = g_ref[...]
     lane = lax.broadcasted_iota(jnp.int32, (1, size), 1)
     line = lax.broadcasted_iota(jnp.int32, (count, 1), 0)
     for base in range(0, size, count):
         below = base + count
-        for q in range(2):
-            block = eliminate(work[q, base:below, :], base, count)
-            lower = lane <= line + base
-            inverse[q, base:below, :] = jnp.where(lower, block, 0.0)
-            if below < size:
-                a, b = spread_pair(block, jnp.where(lower | (lane >= below), block, 0.0))
-                change = dot(a, b, ((0,), (0,)))[below:]
-                panel = (lane >= base) & (lane < below)
-                work[q, below:, :] = jnp.where(panel, 0.0, work[q, below:, :]) - change
-    left_ref[...] = dot(inverse[0], y_ref[...], ((1,), (1,)), lax.Precision.HIGHEST).astype(BF16)
+        block = eliminate(work[base:below, :], base, count)
+        lower = lane <= line + base
+        inverse[base:below, :] = jnp.where(lower, block, 0.0)
+        if below < size:
+            a, b = spread_pair(block, jnp.where(lower | (lane >= below), block, 0.0))
+            change = dot(a, b, ((0,), (0,)))[below:]
+            panel = (lane >= base) & (lane < below)
+            work[below:, :] = jnp.where(panel, 0.0, work[below:, :]) - change
+        yield
+
+
+def take(steps, count):
+    for _ in range(count):
+        next(steps, None)
+
+
+def sum_kernel(rows_total, cols_total, b_ref, p_ref, left_ref, g_ref, w_ref, away, y_home, y_from_k, out_x, from_x, strip, from_z,
+               y_tile, y_rows, coded, y_ref, parts, out, ring, mine, gram, gram1, total1, from_k, home, from_zx, tile, from_y, piece, inverse,
+               y_sends, y_recvs, rs_send, rs_recv, ag_send, ag_recv, sends, recvs):
+    row, k = lax.axis_index("row"), lax.axis_index("k")
+    me = lax.axis_index("z") * NX + lax.axis_index("x")
+    cols = p_ref.shape[0]
+    wait_barrier = greet(("row",), "zx", "k")
+    ex = sum_y(wait_barrier, b_ref, p_ref, y_ref, away, y_home, y_from_k, out_x, from_x, strip, from_z, y_tile, y_rows, coded,
+               y_sends, y_recvs)
+    y = y_ref[...]
+    high = y.astype(BF16)
+    low = (y - high.astype(F32)).astype(BF16)
+    for chunk in range(NY):
+        width = min(256, cols - 256 * chunk)
+        block = p_ref[256 * chunk : 256 * chunk + width, :]
+        value = dot(block, high, ((1,), (0,))) + dot(block, low, ((1,), (0,)))
+        if width < 256:
+            parts[chunk, 128:, :] = jnp.zeros((128, 256), F32)
+        parts[chunk, :width, :] = value
+    reduce = Ring(parts, out, ring, rs_send, rs_recv)
+    reduce.step(0)
+
+    def exchange(axes, source, target):
+        number = len(ex) - 6
+        ex.append(Exchange(axes, source, target, sends.at[number], recvs.at[number]))
+
+    def over_rows(which):
+        ex[-1].arrived()
+        whole = from_y[which, 0]
+        for number in range(1, NY):
+            whole += from_y[which, number]
+        return whole
+
+    gram1[...] = dot(y, y, ((0,), (0,)), lax.Precision.HIGHEST) / rows_total
+    own = gram1[pl.ds(pl.multiple_of(128 * k + 8 * (me // 2), 8), 8), part(lax.rem(me, 2), 128)]
+    tile[0] = own
+    from_y[0, row] = own
+    exchange(("row",), lambda to: tile.at[0], lambda slot: from_y.at[0, row])
+    reduce.step(1)
+    whole = over_rows(0)
+    piece[0] = whole
+    half1 = total1.at[part(k, 128)]
+    tile_of(half1, me, 128)[...] = whole
+    exchange("zx", lambda to: piece.at[0], lambda slot: tile_of(half1, me, 128))
+    reduce.step(2)
+    ex[-1].arrived()
+    exchange("k", lambda to: half1, lambda slot: half1)
+    reduce.step(3)
+    ex[-1].arrived()
+    gram1[...] = total1[...]
+    steps = inverse_steps(gram1, inverse)
+    take(steps, 1)
+    reduce.last(mine)
+    gram[...] = dot(mine[...], mine[...], ((0,), (0,)), lax.Precision.HIGHEST)
+    gather = Gather(w_ref, ag_send, ag_recv)
+    exchange("k", lambda to: gram.at[part(to, 128)], lambda slot: from_k)
+    for half in range(2):
+        encode(mine[pl.ds(128 * half, 128), :], w_ref.at[row, half])
+    gather.step(0)
+    take(steps, 2)
+    ex[-1].arrived()
+    home[...] = gram[part(k, 128), :] + from_k[...]
+    exchange("zx", lambda to: tile_of(home, to, 128), lambda slot: from_zx.at[slot])
+    take(steps, 3)
+    gather.step(1)
+    take(steps, 3)
+    ex[-1].arrived()
+    total = tile_of(home, me, 128)[...]
+    for slot in range(NZ * NX - 1):
+        total += from_zx[slot]
+    tile[1] = total
+    from_y[1, row] = total
+    exchange(("row",), lambda to: tile.at[1], lambda slot: from_y.at[1, row])
+    gather.step(2)
+    take(steps, 5)
+    whole = over_rows(1) / cols_total
+    piece[1] = whole
+    half2 = g_ref.at[part(k, 128)]
+    tile_of(half2, me, 128)[...] = whole
+    exchange("zx", lambda to: piece.at[1], lambda slot: tile_of(half2, me, 128))
+    gather.step(3)
+    take(steps, 16)
+    left_ref[...] = dot(inverse[...], y_ref[...], ((1,), (1,)), lax.Precision.HIGHEST).astype(BF16)
+    ex[-1].arrived()
+    exchange("k", lambda to: half2, lambda slot: half2)
+    gather.step(4)
+    for e in ex:
+        e.sent()
+    ex[-1].arrived()
+    for copy in reduce.waiting + gather.waiting:
+        copy.wait_send()
+
+
+def halves(value):
+    high = value.astype(BF16)
+    return high, (value - high.astype(F32)).astype(BF16)
+
+
+def finish_kernel(g_ref, w_ref, before_ref, right_ref, left_ref, work, inverse, wide):
+    left_ref[...] = before_ref[...]
+    work[...] = g_ref[...]
+    for chunk, _ in enumerate(inverse_steps(work, inverse)):
+        high, low = halves(decode(w_ref[chunk // 2, chunk % 2]))
+        wide[chunk] = jnp.concatenate([high, high, low], 1)
+    high, low = halves(inverse[...])
+    factor = jnp.concatenate([high, low, high], 1)
     cols = right_ref.shape[0]
     for chunk in range(2 * NY):
         width = min(128, cols - 128 * chunk)
-        value = dot(decode(w_ref[chunk // 2, chunk % 2]), inverse[1], ((1,), (1,)), lax.Precision.HIGHEST)
+        value = dot(wide[chunk], factor, ((1,), (1,)))
         right_ref[128 * chunk : 128 * chunk + width, :] = value[:width].astype(BF16)
 
 
@@ -375,60 +429,61 @@
     rows, cols = ppmi.shape
     rows_total, cols_total = rows * NY, cols * NZ * NX * NK
     dma = pltpu.SemaphoreType.DMA
-    params = functools.partial(pltpu.CompilerParams, has_side_effects=True, vmem_limit_bytes=LIMIT)
-    y = pl.pallas_call(
-        y_kernel,
-        out_shape=jax.ShapeDtypeStruct((512, 256), F32),
+    vmem = pltpu.VMEM
+    left, gram, w = pl.pallas_call(
+        functools.partial(sum_kernel, rows_total, cols_total),
+        out_shape=[
+            jax.ShapeDtypeStruct((256, rows), BF16),
+            jax.ShapeDtypeStruct((256, 256), F32),
+            jax.ShapeDtypeStruct((8, 2, 144, 256), BF16),
+        ],
         in_specs=[VMEM] * 2,
-        out_specs=VMEM,
+        out_specs=[VMEM] * 3,
         scratch_shapes=[
-            pltpu.VMEM((256, 256), F32),
-            pltpu.VMEM((256, 256), F32),
-            pltpu.VMEM((256, 256), F32),
-            pltpu.VMEM((3, 64, 256), F32),
-            pltpu.VMEM((64, 256), F32),
-            pltpu.VMEM((7, 8, 256), F32),
-            pltpu.VMEM((8, 256), F32),
+            vmem((256, 256), F32),
+            vmem((256, 256), F32),
+            vmem((256, 256), F32),
+            vmem((4, 80, 256), BF16),
+            vmem((3, 80, 256), BF16),
+            vmem((64, 256), F32),
+            vmem((7, 8, 256), F32),
+            vmem((8, 256), F32),
+            vmem((64, 256), F32),
+            vmem((2, 4, 80, 256), BF16),
+            vmem((512, 256), F32),
+            vmem((8, 256, 256), F32),
+            vmem((4, 2, 2, 144, 256), BF16),
+            vmem((4, 2, 2, 144, 256), BF16),
+            vmem((256, 256), F32),
+            vmem((256, 256), F32),
+            vmem((256, 256), F32),
+            vmem((256, 256), F32),
+            vmem((128, 256), F32),
+            vmem((128, 256), F32),
+            vmem((31, 8, 128), F32),
+            vmem((2, 8, 128), F32),
+            vmem((2, 8, 8, 128), F32),
+            vmem((2, 8, 128), F32),
+            vmem((256, 256), F32),
             dma((6, 7)),
             dma((6, 7)),
-        ],
-        compiler_params=params(collective_id=0),
-    )(basis.T, ppmi.T)
-    gram, w = pl.pallas_call(
-        functools.partial(w_kernel, rows_total, cols_total),
-        out_shape=[jax.ShapeDtypeStruct((2, 256, 256), F32), jax.ShapeDtypeStruct((8, 2, 144, 256), BF16)],
-        in_specs=[VMEM] * 2,
-        out_specs=[VMEM] * 2,
-        scratch_shapes=[
-            pltpu.VMEM((8, 256, 256), F32),
-            pltpu.VMEM((4, 2, 2, 144, 256), BF16),
-            pltpu.VMEM((4, 2, 2, 144, 256), BF16),
-            pltpu.VMEM((256, 256), F32),
-            pltpu.VMEM((256, 256), F32),
-            pltpu.VMEM((256, 256), F32),
-            pltpu.VMEM((128, 256), F32),
-            pltpu.VMEM((128, 256), F32),
-            pltpu.VMEM((31, 8, 128), F32),
-            pltpu.VMEM((2, 8, 128), F32),
-            pltpu.VMEM((8, 2, 8, 128), F32),
-            pltpu.VMEM((2, 8, 128), F32),
             dma((4, 2, 2)),
             dma((4, 2, 2)),
             dma((4, 2, 2)),
             dma((4, 2, 2)),
-            dma((5, 31)),
-            dma((5, 31)),
+            dma((8, 31)),
+            dma((8, 31)),
         ],
-        compiler_params=params(collective_id=1),
-    )(y, ppmi.T)
-    left, right = pl.pallas_call(
+        compiler_params=pltpu.CompilerParams(collective_id=0, has_side_effects=True, vmem_limit_bytes=LIMIT),
+    )(basis.T, ppmi.T)
+    right, left = pl.pallas_call(
         finish_kernel,
-        out_shape=[jax.ShapeDtypeStruct((256, rows), BF16), jax.ShapeDtypeStruct((cols, 256), BF16)],
+        out_shape=[jax.ShapeDtypeStruct((cols, 256), BF16), jax.ShapeDtypeStruct((256, rows), BF16)],
         in_specs=[VMEM] * 3,
         out_specs=[VMEM] * 2,
-        scratch_shapes=[pltpu.VMEM((2, 256, 256), F32), pltpu.VMEM((2, 256, 256), F32)],
+        scratch_shapes=[vmem((256, 256), F32), vmem((256, 256), F32), vmem((16, 128, 768), BF16)],
         compiler_params=pltpu.CompilerParams(vmem_limit_bytes=LIMIT),
-    )(gram, y, w)
+    )(gram, w, left)
     return left, right.T
 
 

time: 114 us -> 102 us (0.89)
  Pallas kernels: 113 us -> 101 us
    pallas_call x3 -> x2, Pallas kernels: 113 us -> 101 us  [the longest x1 86.3 us: local(): pl.pallas_call(functools.partial(sum_kernel, rows_total, cols_total), out...]
where the time goes in v4:
time: 102 us
  Pallas kernels  101 us (99%)
    pallas_call x1, Pallas kernels, local(): pl.pallas_call(functools.partial(sum_kernel, rows_total, cols_total), out...  86.3 us
    pallas_call x1, Pallas kernels, local(): pl.pallas_call(finish_kernel, out_shape=[jax.ShapeDtypeStruct((cols, 256)...  14.6 us

profile of v4, /device:TPU:1, one launch (start us, length us, event | category | flops | bytes accessed | tf_op | source)
XLA Modules:
  0.0 101.5 jit_solution(5425898176415297995)
XLA Ops:
  0.6 86.3 %shard_map.41 = (bf16[256,512]{1,0:T(8,128)(2,1)}, f32[256,256]{1,0:T(8,128)}, bf16[8,2,144,256]{3,2,1,0:T(8,128)(2,1)}) custom-call(bf16[2004,256]{1,0:T(8,128)(2,1)} %bitcast.4, bf16[2004,512]{1,0:T(8,128)(2,1)} %bitcast.3), custom_call_target="tpu_custom_call" | custom-call | tf_op jit(solution)/shard_map/pallas_call | solution.py:433
  86.9 14.6 %shard_map.42 = (bf16[2004,256]{1,0:T(8,128)(2,1)}, bf16[256,512]{1,0:T(8,128)(2,1)}) custom-call(f32[256,256]{1,0:T(8,128)} %get-tuple-element.7.g_ref, bf16[8,2,144,256]{3,2,1,0:T(8,128)(2,1)} %get-tuple-element.8.w_ref, bf16[256,512]{1,0:T(8,128)(2,1)} %get-tuple-element.9.before_ref), custom_call_target="tpu_custom_call" | custom-call | tf_op jit(solution)/shard_map/pallas_call | solution.py:479

commit v5 on v4

--- a/solution.py
+++ b/solution.py
@@ -16,6 +16,9 @@
 SIZES = {"row": NY, "z": NZ, "x": NX, "k": NK}
 VMEM = pl.BlockSpec(memory_space=pltpu.VMEM)
 LIMIT = 56 << 20
+COUNT = 32
+LATE = 1
+CUT = 1
 
 
 def peer(axis, step):
@@ -290,8 +293,8 @@
     return jnp.concatenate([jnp.concatenate(tiles[h], 0) for h in range(2)], 1)
 
 
-def inverse_steps(work, inverse):
-    size, count = 256, 16
+def inverse_steps(work, inverse, count=16):
+    size = 256
     lane = lax.broadcasted_iota(jnp.int32, (1, size), 1)
     line = lax.broadcasted_iota(jnp.int32, (count, 1), 0)
     for base in range(0, size, count):
@@ -301,7 +304,8 @@
         inverse[base:below, :] = jnp.where(lower, block, 0.0)
         if below < size:
             a, b = spread_pair(block, jnp.where(lower | (lane >= below), block, 0.0))
-            change = dot(a, b, ((0,), (0,)))[below:]
+            skip = below // 128 * 128 if CUT else 0
+            change = dot(a[:, skip:], b, ((0,), (0,)))[below - skip :]
             panel = (lane >= base) & (lane < below)
             work[below:, :] = jnp.where(panel, 0.0, work[below:, :]) - change
         yield
@@ -385,13 +389,17 @@
     tile[1] = total
     from_y[1, row] = total
     exchange(("row",), lambda to: tile.at[1], lambda slot: from_y.at[1, row])
-    gather.step(2)
+    if not LATE:
+        gather.step(2)
     take(steps, 5)
     whole = over_rows(1) / cols_total
     piece[1] = whole
     half2 = g_ref.at[part(k, 128)]
     tile_of(half2, me, 128)[...] = whole
     exchange("zx", lambda to: piece.at[1], lambda slot: tile_of(half2, me, 128))
+    if LATE:
+        gather.step(2)
+        take(steps, 2)
     gather.step(3)
     take(steps, 16)
     left_ref[...] = dot(inverse[...], y_ref[...], ((1,), (1,)), lax.Precision.HIGHEST).astype(BF16)
@@ -413,9 +421,10 @@
 def finish_kernel(g_ref, w_ref, before_ref, right_ref, left_ref, work, inverse, wide):
     left_ref[...] = before_ref[...]
     work[...] = g_ref[...]
-    for chunk, _ in enumerate(inverse_steps(work, inverse)):
-        high, low = halves(decode(w_ref[chunk // 2, chunk % 2]))
-        wide[chunk] = jnp.concatenate([high, high, low], 1)
+    for number, _ in enumerate(inverse_steps(work, inverse, COUNT)):
+        for chunk in range(number * COUNT // 16, (number + 1) * COUNT // 16):
+            high, low = halves(decode(w_ref[chunk // 2, chunk % 2]))
+            wide[chunk] = jnp.concatenate([high, high, low], 1)
     high, low = halves(inverse[...])
     factor = jnp.concatenate([high, low, high], 1)
     cols = right_ref.shape[0]

time: 102 us -> 100 us (0.980)
  Pallas kernels: 101 us -> 98.7 us
    pallas_call x1, Pallas kernels: 14.6 us -> 13.4 us  [local(): pl.pallas_call(finish_kernel, out_shape=[jax.ShapeDtypeStruct((cols, 256)...]
    pallas_call x1, Pallas kernels: 86.3 us -> 85.3 us  [local(): pl.pallas_call(functools.partial(sum_kernel, rows_total, cols_total), out...]
where the time goes in v5:
time: 100 us; the launch traced here: 99.3 us
  Pallas kernels  98.7 us (99%)
    pallas_call x1, Pallas kernels, local(): pl.pallas_call(functools.partial(sum_kernel, rows_total, cols_total), out...  85.3 us
    pallas_call x1, Pallas kernels, local(): pl.pallas_call(finish_kernel, out_shape=[jax.ShapeDtypeStruct((cols, 256)...  13.4 us

profile of v5, /device:TPU:1, one launch (start us, length us, event | category | flops | bytes accessed | tf_op | source)
XLA Modules:
  0.0 99.3 jit_solution(15593022116349958818)
XLA Ops:
  0.6 85.3 %shard_map.41 = (bf16[256,512]{1,0:T(8,128)(2,1)}, f32[256,256]{1,0:T(8,128)}, bf16[8,2,144,256]{3,2,1,0:T(8,128)(2,1)}) custom-call(bf16[2004,256]{1,0:T(8,128)(2,1)} %bitcast.4, bf16[2004,512]{1,0:T(8,128)(2,1)} %bitcast.3), custom_call_target="tpu_custom_call" | custom-call | tf_op jit(solution)/shard_map/pallas_call | solution.py:442
  85.9 13.4 %shard_map.42 = (bf16[2004,256]{1,0:T(8,128)(2,1)}, bf16[256,512]{1,0:T(8,128)(2,1)}) custom-call(f32[256,256]{1,0:T(8,128)} %get-tuple-element.7.g_ref, bf16[8,2,144,256]{3,2,1,0:T(8,128)(2,1)} %get-tuple-element.8.w_ref, bf16[256,512]{1,0:T(8,128)(2,1)} %get-tuple-element.9.before_ref), custom_call_target="tpu_custom_call" | custom-call | tf_op jit(solution)/shard_map/pallas_call | solution.py:488
